TPU v7x, 128 devices: a whole 4x4x4 slice. The times are simulated.
128 devices in a mesh: seq: 32 (over x, z, core), tp: 4 (over y).
Axes of the slice: x: 4, y: 4, z: 4, core: 2. Of those that a mesh axis runs over, the one named last changes fastest.
Arguments:
- residual: bfloat16 [1024, 2560], P('seq', 'tp'), may hold values from -6 to 6
- queries: bfloat16 [1024, 3072], P('seq', 'tp'), may hold values from -80 to 80
- new_kv: bfloat16 [1024, 512], P('seq'), may hold values from -8 to 8
- cache: bfloat16 [2048, 256, 512], P('seq'), may hold values from -8 to 8
- out_weight: bfloat16 [3072, 2560], P('tp'), may hold values from -0.109375 to 0.109375
- block_counts: int32 [1024], replicated, may hold values from 1 to 8, 2048 in all
- last_fill: int32 [1024], replicated, may hold values from 1 to 256
- block_order: int32 [2048], P('seq'), may hold values from 0 to 2047, each once
Outputs:
- layer_out: bfloat16 [1024, 2560], P('seq', 'tp')
Inputs may be any that keep to these rules, and one draw needn't show every extreme that they name: block_counts sums to 2048, and some request has 8 blocks. last_fill of a request is the live tokens of its last block; all its other blocks are full. block_order is a permutation of the pool entries.
All inputs are finite; a program needn't handle non-finite values.
Results may differ from a plain program's by a relative error of at most 0.012.
Values may be sent and summed in bfloat16 or wider, within the bound.
A program may use at most 256 MiB of HBM per device.

v0:
```python
import jax
import jax.numpy as jnp
from jax import lax
from jax.sharding import PartitionSpec as P

very_low = -1e30


def place_blocks(block_counts, block_order):
    num_req = block_counts.shape[0]
    ends = jnp.cumsum(block_counts)
    pool_start = ends - block_counts
    block_req = jnp.sum((pool_start[None, :] <= block_order[:, None]).astype(jnp.int32), axis=1) - 1
    onehot = block_req[:, None] == jnp.arange(num_req, dtype=jnp.int32)[None, :]
    start_here = jnp.sum(jnp.where(onehot, pool_start[None, :], 0), axis=1)
    count_here = jnp.sum(jnp.where(onehot, block_counts[None, :], 0), axis=1)
    return (block_req, block_order - start_here, count_here, onehot)


def request_table(block_max, block_sum, block_acc, block_req, onehot):
    num_blocks, heads_here, head_dim = block_acc.shape
    num_req = onehot.shape[1]
    same_req = block_req[:, None] == block_req[None, :]
    max_at_block = jnp.max(jnp.where(same_req[:, :, None], block_max[None, :, :], very_low), axis=1)
    factor = jnp.exp(block_max - max_at_block)
    member = onehot.T
    cache_max = jnp.max(jnp.where(member[:, :, None], block_max[None, :, :], very_low), axis=1)
    member_float = member.astype(jnp.float32)
    cache_sum = jnp.dot(member_float, block_sum * factor, precision=lax.Precision.HIGHEST)
    scaled_acc = (block_acc * factor[:, :, None]).reshape(num_blocks, heads_here * head_dim)
    cache_acc = jnp.dot(member_float, scaled_acc, precision=lax.Precision.HIGHEST).reshape(
        num_req, heads_here, head_dim
    )
    return (cache_max, cache_sum, cache_acc)


def local(residual, queries, new_kv, cache, out_weight, block_counts, last_fill, block_order):
    rows_here = residual.shape[0]
    width_here = residual.shape[1]
    head_dim = new_kv.shape[1] // 2
    heads_here = queries.shape[1] // head_dim
    block_len = cache.shape[1]
    num_blocks = cache.shape[0]
    inv_root = 1.0 / head_dim**0.5
    query_all = lax.all_gather(queries, "seq", axis=0, tiled=True)
    block_req, block_slot, count_here, onehot = place_blocks(block_counts, block_order)
    fill_here = jnp.sum(jnp.where(onehot, last_fill[None, :], 0), axis=1)
    live_mask = (block_slot < count_here - 1)[:, None] | (
        jnp.arange(block_len, dtype=jnp.int32)[None, :] < fill_here[:, None]
    )
    query_blocks = query_all[block_req].reshape(num_blocks, heads_here, head_dim)
    keys = cache[:, :, :head_dim]
    values = cache[:, :, head_dim:]
    scores = (
        jnp.einsum("bhd,btd->bht", query_blocks, keys, preferred_element_type=jnp.float32)
        * inv_root
    )
    scores = jnp.where(live_mask[:, None, :], scores, very_low)
    block_max = jnp.max(scores, axis=2)
    weights = jnp.where(live_mask[:, None, :], jnp.exp(scores - block_max[:, :, None]), 0.0)
    block_sum = jnp.sum(weights, axis=2)
    rounded = weights.astype(jnp.bfloat16)
    block_acc = jnp.einsum("bht,btd->bhd", rounded, values, preferred_element_type=jnp.float32)
    cache_max, cache_sum, cache_acc = request_table(
        block_max, block_sum, block_acc, block_req, onehot
    )
    got_max, got_sum, got_acc = (
        lax.all_to_all(cache_max, "seq", split_axis=0, concat_axis=0, tiled=True),
        lax.all_to_all(cache_sum, "seq", split_axis=0, concat_axis=0, tiled=True),
        lax.all_to_all(cache_acc, "seq", split_axis=0, concat_axis=0, tiled=True),
    )
    sources = got_max.shape[0] // rows_here
    got_max = got_max.reshape(sources, rows_here, heads_here)
    got_sum = got_sum.reshape(sources, rows_here, heads_here)
    got_acc = got_acc.reshape(sources, rows_here, heads_here, head_dim)
    home_max = jnp.max(got_max, axis=0)
    source_factor = jnp.exp(got_max - home_max[None, :, :])
    home_sum = jnp.sum(got_sum * source_factor, axis=0)
    home_acc = jnp.sum(got_acc * source_factor[:, :, :, None], axis=0)
    query_home = queries.reshape(rows_here, heads_here, head_dim)
    own_score = (
        jnp.einsum(
            "rhd,rd->rh", query_home, new_kv[:, :head_dim], preferred_element_type=jnp.float32
        )
        * inv_root
    )
    top_score = jnp.maximum(home_max, own_score)
    cache_factor = jnp.exp(home_max - top_score)
    own_factor = jnp.exp(own_score - top_score)
    denominator = home_sum * cache_factor + own_factor
    new_value = new_kv[:, head_dim:].astype(jnp.float32)
    mixed_sum = home_acc * cache_factor[:, :, None] + own_factor[:, :, None] * new_value[:, None, :]
    attention = (
        (mixed_sum / denominator[:, :, None])
        .reshape(rows_here, heads_here * head_dim)
        .astype(jnp.bfloat16)
    )
    partial_out = jnp.dot(attention, out_weight, preferred_element_type=jnp.float32)
    summed = lax.psum(partial_out.astype(jnp.bfloat16), "tp").astype(jnp.float32)
    columns = lax.dynamic_slice_in_dim(summed, lax.axis_index("tp") * width_here, width_here, 1)
    return (residual.astype(jnp.float32) + columns).astype(jnp.bfloat16)


def solution(mesh):
    in_specs = (
        P("seq", "tp"),
        P("seq", "tp"),
        P("seq", None),
        P("seq", None, None),
        P("tp", None),
        P(),
        P(),
        P("seq"),
    )
    out_specs = P("seq", "tp")
    return jax.shard_map(local, mesh=mesh, in_specs=in_specs, out_specs=out_specs, check_vma=False)
```

profile of v0, /device:TPU:0, one launch (start us, length us, event | category | flops | bytes accessed | tf_op | source)
XLA Modules:
  0.0 207.6 jit_solution(12501185500906286605)
XLA Ops:
  6.5 0.7 all-gather.2.cloned.1.call-update
  7.3 1.0 reduce-window.9
  8.4 0.8 bitcast_subtract_fusion
  9.2 0.8 convert_reduce_fusion
  10.1 1.0 select_reduce_fusion.3
  11.1 0.7 add_compare_fusion
  12.0 43.5 %all-gather.2.cloned.1.call-done = bf16[1024,768]{1,0:T(8,128)(2,1)} async-done(((bf16[32,768]{1,0:T(8,128)(2,1)}), bf16[1024,768]{1,0:T(8,128)(2,1)}) %all-gather.2.cloned.1.call-update) | async-done | bytes 1572880 | tf_op jit(solution)/shard_map/all_gather | solution.py:45
  55.5 2.4 %gather_fusion = bf16[64,768]{1,0:T(8,128)(2,1)S(1)} fusion(bf16[1024,768]{1,0:T(8,128)(2,1)} %all-gather.2.cloned.1.call-done, s32[1024]{0:T(1024)S(1)} %pad_clamp_fusion), kind=kCustom, calls=%fused_computation | custom fusion | bytes 196864 | tf_op jit(solution)/shard_map/gather | solution.py:51
  57.9 5.7 %fusion.42 = (f32[64,3]{1,0:T(8,128)S(1)}, f32[64,3,256]{2,1,0:T(4,128)S(1)}) fusion(bf16[64,3,256]{2,1,0:T(4,128)(2,1)S(1)} %reshape.170, bf16[64,256,512]{2,1,0:T(8,128)(2,1)} %param.11, pred[64,256]{1,0:T(8,128)(4,1)S(1)} %fusion.28), kind=kOutput, calls=%fused_computation.62 | convolution fusion | flops 25313088 | bytes 8700672 | tf_op jit(solution)/shard_map/bhd,btd->bht/dot_general | solution.py:55
  64.2 4.6 %fusion.8 = f32[64,3,256]{2,1,0:T(4,128)S(1)} fusion(bf16[64,256,512]{2,1,0:T(8,128)(2,1)} %param.11, f32[64,3,256]{2,1,0:T(4,128)S(1)} %get-tuple-element.16, f32[64,3]{1,0:T(8,128)S(1)} %subtract_exponential_fusion, f32[64,3]{1,0:T(8,128)S(1)} %get-tuple-element.15, pred[64,256]{1,0:T(8,128)(4,1)S(1)} %fusion.28), kind=kOutput, calls=%fused_computation.9 | convolution fusion | flops 25362432 | bytes 8799744 | tf_op jit(solution)/shard_map/bht,btd->bhd/dot_general | solution.py:63
  69.2 0.7 copy.63
  69.9 5.2 %all-to-all-start.2 = ((f32[32,32,3]{1,2,0:T(4,128)}), f32[32,32,3]{1,2,0:T(4,128)S(1)}, u32[]{:S(2)}, u32[]{:S(2)}) async-start(f32[32,32,3]{1,2,0:T(4,128)} %copy.63), calls=%async_computation.2 | async-start | bytes 131072 | tf_op jit(solution)/shard_map/all_to_all | solution.py:69
  75.3 0.7 copy.59
  76.0 6.6 %all-to-all-done.2 = f32[32,32,3]{1,2,0:T(4,128)S(1)} async-done(((f32[32,32,3]{1,2,0:T(4,128)}), f32[32,32,3]{1,2,0:T(4,128)S(1)}, u32[]{:S(2)}, u32[]{:S(2)}) %all-to-all-start.2) | async-done | bytes 12320 | tf_op jit(solution)/shard_map/all_to_all | solution.py:69
  82.6 3.8 %all-to-all-start.1 = ((f32[32,32,3]{1,2,0:T(4,128)}), f32[32,32,3]{1,2,0:T(4,128)S(1)}, u32[]{:S(2)}, u32[]{:S(2)}) async-start(f32[32,32,3]{1,2,0:T(4,128)} %copy.59), calls=%async_computation.1 | async-start | bytes 131072 | tf_op jit(solution)/shard_map/all_to_all | solution.py:68
  86.5 1.5 fusion.16
  88.0 4.1 %copy.57 = f32[1024,3,256]{2,1,0:T(4,128)} copy(f32[1024,3,256]{2,0,1:T(8,128)S(1)} %fusion.16) | data formatting | bytes 6291456 | tf_op jit(solution)/shard_map/dot_general | solution.py:31
  92.1 1.9 all-to-all-done.1
  94.0 5.7 %all-to-all-start = ((f32[1024,3,256]{2,1,0:T(4,128)}), f32[1024,3,256]{2,1,0:T(4,128)}, u32[]{:S(2)}, u32[]{:S(2)}) async-start(f32[1024,3,256]{2,1,0:T(4,128)} %copy.57), calls=%async_computation | async-start | bytes 8388608 | tf_op jit(solution)/shard_map/all_to_all | solution.py:70
  100.2 52.3 %all-to-all-done = f32[1024,3,256]{2,1,0:T(4,128)} async-done(((f32[1024,3,256]{2,1,0:T(4,128)}), f32[1024,3,256]{2,1,0:T(4,128)}, u32[]{:S(2)}, u32[]{:S(2)}) %all-to-all-start) | async-done | bytes 3145760 | tf_op jit(solution)/shard_map/all_to_all | solution.py:70
  152.5 2.9 %fusion.4 = f32[32,3,256]{2,0,1:T(8,128)S(1)} fusion(f32[32,32,3,256]{3,2,1,0:T(4,128)} %bitcast.7, f32[32,32,3]{1,0,2:T(8,128)S(1)} %get-tuple-element.12), kind=kLoop, calls=%fused_computation.7 | loop fusion | flops 1548288 | bytes 3256320 | tf_op jit(solution)/shard_map/reduce_sum | solution.py:79
  155.9 1.4 convolution_convert_fusion
  157.3 42.0 %all-reduce.2.cloned.1.call-done = bf16[32,2560]{1,0:T(8,128)(2,1)} async-done(((bf16[32,2560]{1,0:T(8,128)(2,1)}), bf16[32,2560]{1,0:T(8,128)(2,1)}) %all-reduce.2.cloned.1.call-update) | async-done | bytes 163856 | tf_op jit(solution)/shard_map/psum | solution.py:99
  199.3 1.4 add_convert_fusion
  (39 shorter events, 2.6 us)
Async XLA Ops:
  6.5 49.0 %all-gather.2.cloned.1.call-start = ((), (), s32[]{:S(2)}) async-start(), calls=%async_computation.3 | async-start | bytes 1622016 | tf_op jit(solution)/shard_map/all_gather | solution.py:45
  69.9 12.7 %all-to-all-start.2 = ((f32[32,32,3]{1,2,0:T(4,128)}), f32[32,32,3]{1,2,0:T(4,128)S(1)}, u32[]{:S(2)}, u32[]{:S(2)}) async-start(f32[32,32,3]{1,2,0:T(4,128)} %copy.63), calls=%async_computation.2 | async-start | bytes 131072 | tf_op jit(solution)/shard_map/all_to_all | solution.py:69
  82.6 11.4 %all-to-all-start.1 = ((f32[32,32,3]{1,2,0:T(4,128)}), f32[32,32,3]{1,2,0:T(4,128)S(1)}, u32[]{:S(2)}, u32[]{:S(2)}) async-start(f32[32,32,3]{1,2,0:T(4,128)} %copy.59), calls=%async_computation.1 | async-start | bytes 131072 | tf_op jit(solution)/shard_map/all_to_all | solution.py:68
  92.1 7.7 %copy-start.1 = (bf16[32,768]{1,0:T(8,128)(2,1)S(1)}, bf16[32,768]{1,0:T(8,128)(2,1)}, u32[]{:S(2)}) copy-start(bf16[32,768]{1,0:T(8,128)(2,1)} %param.9) | copy-start | bytes 147460
  92.1 7.7 %copy-start.3 = (bf16[32,512]{1,0:T(8,128)(2,1)S(1)}, bf16[32,512]{1,0:T(8,128)(2,1)}, u32[]{:S(2)}) copy-start(bf16[32,512]{1,0:T(8,128)(2,1)} %param.10) | copy-start | bytes 98308
  94.0 58.5 %all-to-all-start = ((f32[1024,3,256]{2,1,0:T(4,128)}), f32[1024,3,256]{2,1,0:T(4,128)}, u32[]{:S(2)}, u32[]{:S(2)}) async-start(f32[1024,3,256]{2,1,0:T(4,128)} %copy.57), calls=%async_computation | async-start | bytes 8388608 | tf_op jit(solution)/shard_map/all_to_all | solution.py:70
  99.7 99.6 %all-reduce.2.cloned.1.call-start = ((), (), s32[]{:S(2)}) async-start(), calls=%async_computation.4 | async-start | bytes 327680 | tf_op jit(solution)/shard_map/psum | solution.py:99
  152.5 3.4 %copy-start = (bf16[768,2560]{1,0:T(8,128)(2,1)S(1)}, bf16[768,2560]{1,0:T(8,128)(2,1)}, u32[]{:S(2)}) copy-start(bf16[768,2560]{1,0:T(8,128)(2,1)} %param.12) | copy-start | bytes 11796484
  152.5 46.8 %copy-start.2 = (bf16[32,640]{1,0:T(8,128)(2,1)S(1)}, bf16[32,640]{1,0:T(8,128)(2,1)}, u32[]{:S(2)}) copy-start(bf16[32,640]{1,0:T(8,128)(2,1)} %param.8) | copy-start | bytes 122884
Sparse Core Ops, SparseCore 0:
  9.6 45.8 all-gather.1
  157.5 41.8 all-reduce.1
where the time goes:
time: 208 us
  waiting for transfers between devices  147 us (71%)
  starting transfers between devices  14.8 us (7%)
  matrix products  13.7 us (7%)
  between operations  13.6 us (7%)
  other arithmetic  9.63 us (5%)
  local copies, waits for them, and re-layouts  8.82 us (4%)
    all_to_all x1, waiting for transfers between devices, local(): lax.all_to_all(cache_acc, 'seq', split_axis=0, concat_axis=0, tiled=True)  52.3 us
    all_gather x1, waiting for transfers between devices, local(): query_all = lax.all_gather(queries, 'seq', axis=0, tiled=True)  43.5 us
    psum x1, waiting for transfers between devices, local(): lax.psum(partial_out.astype(jnp.bfloat16), 'tp').astype(jnp.float32)  42 us
    all_to_all x1, waiting for transfers between devices, local(): lax.all_to_all(cache_sum, 'seq', split_axis=0, concat_axis=0, tiled=True)  6.6 us
    dot_general x1, matrix products, local(): jnp.einsum('bhd,btd->bht', query_blocks, keys, preferred_element_type=jnp...  5.73 us
    all_to_all x1, starting transfers between devices, local(): lax.all_to_all(cache_acc, 'seq', split_axis=0, concat_axis=0, tiled=True)  5.73 us
    all_to_all x1, starting transfers between devices, local(): lax.all_to_all(cache_sum, 'seq', split_axis=0, concat_axis=0, tiled=True)  5.18 us
    dot_general x1, matrix products, local(): jnp.einsum('bht,btd->bhd', rounded, values, preferred_element_type=jnp.fl...  4.62 us
  transfers between devices with their start and end apart: 5, of which 5 were waited for; matrix products, arithmetic and copies ran while one was open for 6% of the time, Pallas kernels for 0%

commit v1 on v0

--- a/solution.py
+++ b/solution.py
@@ -42,7 +42,8 @@
     block_len = cache.shape[1]
     num_blocks = cache.shape[0]
     inv_root = 1.0 / head_dim**0.5
-    query_all = lax.all_gather(queries, "seq", axis=0, tiled=True)
+    stack = jnp.stack([queries] * lax.axis_size("seq"))
+    query_all = jnp.concatenate(lax.all_to_all(stack, "seq", 0, 0), axis=0)
     block_req, block_slot, count_here, onehot = place_blocks(block_counts, block_order)
     fill_here = jnp.sum(jnp.where(onehot, last_fill[None, :], 0), axis=1)
     live_mask = (block_slot < count_here - 1)[:, None] | (

time: 208 us -> 190 us (0.913)
  waiting for transfers between devices: 147 us -> 125 us
  starting transfers between devices: 14.8 us -> 21.7 us
  other arithmetic: 9.63 us -> 6.23 us
    all_gather x1 -> x0, waiting for transfers between devices: 43.5 us -> none  [local(): query_all = lax.all_gather(queries, 'seq', axis=0, tiled=True)]
    all_to_all x0 -> x1, waiting for transfers between devices: none -> 21.7 us  [local(): query_all = jnp.concatenate(lax.all_to_all(stack, 'seq', 0, 0), axis=0)]
    all_to_all x0 -> x1, starting transfers between devices: none -> 8.24 us  [local(): query_all = jnp.concatenate(lax.all_to_all(stack, 'seq', 0, 0), axis=0)]
    another operation x1 -> x2, local copies, waits for them, and re-layouts: 0.12 us -> 2.29 us  [the longest x1 2.17 us: local(): stack = jnp.stack([queries] * lax.axis_size('seq'))]
  transfers between devices with their start and end apart: 5 -> 5, of which waited for: 5 -> 5; matrix products, arithmetic and copies ran while one was open for 6% -> 4% of each run, Pallas kernels for 0% -> 0%
where the time goes in v1:
time: 190 us; the launch traced here: 189 us
  waiting for transfers between devices  125 us (66%)
  starting transfers between devices  21.7 us (11%)
  matrix products  13.7 us (7%)
  between operations  13.6 us (7%)
  local copies, waits for them, and re-layouts  9.34 us (5%)
  other arithmetic  6.23 us (3%)
    all_to_all x1, waiting for transfers between devices, local(): lax.all_to_all(cache_acc, 'seq', split_axis=0, concat_axis=0, tiled=True)  52.3 us
    psum x1, waiting for transfers between devices, local(): lax.psum(partial_out.astype(jnp.bfloat16), 'tp').astype(jnp.float32)  42.2 us
    all_to_all x1, waiting for transfers between devices, local(): query_all = jnp.concatenate(lax.all_to_all(stack, 'seq', 0, 0), axis=0)  21.7 us
    all_to_all x1, starting transfers between devices, local(): query_all = jnp.concatenate(lax.all_to_all(stack, 'seq', 0, 0), axis=0)  8.24 us
    all_to_all x1, waiting for transfers between devices, local(): lax.all_to_all(cache_sum, 'seq', split_axis=0, concat_axis=0, tiled=True)  6.6 us
    dot_general x1, matrix products, local(): jnp.einsum('bhd,btd->bht', query_blocks, keys, preferred_element_type=jnp...  5.73 us
    all_to_all x1, starting transfers between devices, local(): lax.all_to_all(cache_acc, 'seq', split_axis=0, concat_axis=0, tiled=True)  5.73 us
    dot_general x1, matrix products, local(): jnp.einsum('bht,btd->bhd', rounded, values, preferred_element_type=jnp.fl...  4.62 us
  transfers between devices with their start and end apart: 5, of which 5 were waited for; matrix products, arithmetic and copies ran while one was open for 4% of the time, Pallas kernels for 0%

profile of v1, /device:TPU:0, one launch (start us, length us, event | category | flops | bytes accessed | tf_op | source)
XLA Modules:
  0.0 189.4 jit_solution(5744483446457195897)
XLA Ops:
  6.5 2.2 %stack.2 = bf16[32,32,768]{2,1,0:T(8,128)(2,1)} broadcast(bf16[32,768]{1,0:T(8,128)(2,1)} %param.9), dimensions={1,2} | broadcast | bytes 1622016 | tf_op jit(solution)/shard_map/stack | solution.py:45
  8.7 8.2 %all-to-all-start = ((bf16[32,32,768]{2,1,0:T(8,128)(2,1)}), bf16[32,32,768]{2,1,0:T(8,128)(2,1)S(1)}, u32[]{:S(2)}, u32[]{:S(2)}) async-start(bf16[32,32,768]{2,1,0:T(8,128)(2,1)} %stack.2), calls=%async_computation | async-start | bytes 3145728 | tf_op jit(solution)/shard_map/all_to_all | solution.py:46
  17.0 0.3 reduce-window.9
  18.4 21.7 %all-to-all-done = bf16[32,32,768]{2,1,0:T(8,128)(2,1)S(1)} async-done(((bf16[32,32,768]{2,1,0:T(8,128)(2,1)}), bf16[32,32,768]{2,1,0:T(8,128)(2,1)S(1)}, u32[]{:S(2)}, u32[]{:S(2)}) %all-to-all-start) | async-done | bytes 1572896 | tf_op jit(solution)/shard_map/all_to_all | solution.py:46
  40.1 0.7 gather_fusion
  40.9 5.7 %fusion.42 = (f32[64,3]{1,0:T(8,128)S(1)}, f32[64,3,256]{2,1,0:T(4,128)S(1)}) fusion(bf16[64,3,256]{2,1,0:T(4,128)(2,1)S(1)} %reshape.176, bf16[64,256,512]{2,1,0:T(8,128)(2,1)} %param.11, pred[64,256]{1,0:T(8,128)(4,1)S(1)} %fusion.28), kind=kOutput, calls=%fused_computation.62 | convolution fusion | flops 25313088 | bytes 8700672 | tf_op jit(solution)/shard_map/bhd,btd->bht/dot_general | solution.py:56
  46.7 0.3 fusion.20
  47.2 4.6 %fusion.8 = f32[64,3,256]{2,1,0:T(4,128)S(1)} fusion(bf16[64,256,512]{2,1,0:T(8,128)(2,1)} %param.11, f32[64,3,256]{2,1,0:T(4,128)S(1)} %get-tuple-element.16, f32[64,3]{1,0:T(8,128)S(1)} %subtract_exponential_fusion, f32[64,3]{1,0:T(8,128)S(1)} %get-tuple-element.15, pred[64,256]{1,0:T(8,128)(4,1)S(1)} %fusion.28), kind=kOutput, calls=%fused_computation.9 | convolution fusion | flops 25362432 | bytes 8799744 | tf_op jit(solution)/shard_map/bht,btd->bhd/dot_general | solution.py:64
  51.8 0.3 fusion.14
  52.2 0.7 copy.63
  52.8 3.9 %all-to-all-start.3 = ((f32[32,32,3]{1,2,0:T(4,128)}), f32[32,32,3]{1,2,0:T(4,128)S(1)}, u32[]{:S(2)}, u32[]{:S(2)}) async-start(f32[32,32,3]{1,2,0:T(4,128)} %copy.63), calls=%async_computation.3 | async-start | bytes 131072 | tf_op jit(solution)/shard_map/all_to_all | solution.py:70
  57.0 0.7 copy.59
  57.6 6.6 %all-to-all-done.3 = f32[32,32,3]{1,2,0:T(4,128)S(1)} async-done(((f32[32,32,3]{1,2,0:T(4,128)}), f32[32,32,3]{1,2,0:T(4,128)S(1)}, u32[]{:S(2)}, u32[]{:S(2)}) %all-to-all-start.3) | async-done | bytes 12320 | tf_op jit(solution)/shard_map/all_to_all | solution.py:70
  64.2 3.8 %all-to-all-start.2 = ((f32[32,32,3]{1,2,0:T(4,128)}), f32[32,32,3]{1,2,0:T(4,128)S(1)}, u32[]{:S(2)}, u32[]{:S(2)}) async-start(f32[32,32,3]{1,2,0:T(4,128)} %copy.59), calls=%async_computation.2 | async-start | bytes 131072 | tf_op jit(solution)/shard_map/all_to_all | solution.py:69
  68.1 1.5 fusion.16
  69.6 4.1 %copy.57 = f32[1024,3,256]{2,1,0:T(4,128)} copy(f32[1024,3,256]{2,0,1:T(8,128)S(1)} %fusion.16) | data formatting | bytes 6291456 | tf_op jit(solution)/shard_map/dot_general | solution.py:31
  73.7 1.9 %all-to-all-done.2 = f32[32,32,3]{1,2,0:T(4,128)S(1)} async-done(((f32[32,32,3]{1,2,0:T(4,128)}), f32[32,32,3]{1,2,0:T(4,128)S(1)}, u32[]{:S(2)}, u32[]{:S(2)}) %all-to-all-start.2) | async-done | bytes 12320 | tf_op jit(solution)/shard_map/all_to_all | solution.py:69
  75.6 5.7 %all-to-all-start.1 = ((f32[1024,3,256]{2,1,0:T(4,128)}), f32[1024,3,256]{2,1,0:T(4,128)}, u32[]{:S(2)}, u32[]{:S(2)}) async-start(f32[1024,3,256]{2,1,0:T(4,128)} %copy.57), calls=%async_computation.1 | async-start | bytes 8388608 | tf_op jit(solution)/shard_map/all_to_all | solution.py:71
  81.8 52.3 %all-to-all-done.1 = f32[1024,3,256]{2,1,0:T(4,128)} async-done(((f32[1024,3,256]{2,1,0:T(4,128)}), f32[1024,3,256]{2,1,0:T(4,128)}, u32[]{:S(2)}, u32[]{:S(2)}) %all-to-all-start.1) | async-done | bytes 3145760 | tf_op jit(solution)/shard_map/all_to_all | solution.py:71
  134.1 2.9 %fusion.4 = f32[32,3,256]{2,0,1:T(8,128)S(1)} fusion(f32[32,32,3,256]{3,2,1,0:T(4,128)} %bitcast.8, f32[32,32,3]{1,0,2:T(8,128)S(1)} %get-tuple-element.12), kind=kLoop, calls=%fused_computation.7 | loop fusion | flops 1548288 | bytes 3256320 | tf_op jit(solution)/shard_map/reduce_sum | solution.py:80
  137.2 0.3 copy-done
  137.5 1.4 convolution_convert_fusion
  139.0 42.2 %all-reduce.2.cloned.1.call-done = bf16[32,2560]{1,0:T(8,128)(2,1)} async-done(((bf16[32,2560]{1,0:T(8,128)(2,1)}), bf16[32,2560]{1,0:T(8,128)(2,1)}) %all-reduce.2.cloned.1.call-update) | async-done | bytes 163856 | tf_op jit(solution)/shard_map/psum | solution.py:100
  181.2 1.4 add_convert_fusion
  (45 shorter events, 2.3 us)
Async XLA Ops:
  6.5 10.4 %copy-start.3 = (s32[1024]{0:T(1024)S(1)}, s32[1024]{0:T(1024)}, u32[]{:S(2)}) copy-start(s32[1024]{0:T(1024)} %param.13) | copy-start | bytes 12292
  6.5 11.0 %copy-start.6 = (s32[64]{0:T(128)S(1)}, s32[64]{0:T(128)}, u32[]{:S(2)}) copy-start(s32[64]{0:T(128)} %param.15) | copy-start | bytes 772
  6.5 11.2 %copy-start.5 = (s32[1024]{0:T(1024)S(1)}, s32[1024]{0:T(1024)}, u32[]{:S(2)}) copy-start(s32[1024]{0:T(1024)} %param.14) | copy-start | bytes 12292
  8.7 31.4 %all-to-all-start = ((bf16[32,32,768]{2,1,0:T(8,128)(2,1)}), bf16[32,32,768]{2,1,0:T(8,128)(2,1)S(1)}, u32[]{:S(2)}, u32[]{:S(2)}) async-start(bf16[32,32,768]{2,1,0:T(8,128)(2,1)} %stack.2), calls=%async_computation | async-start | bytes 3145728 | tf_op jit(solution)/shard_map/all_to_all | solution.py:46
  52.8 11.4 %all-to-all-start.3 = ((f32[32,32,3]{1,2,0:T(4,128)}), f32[32,32,3]{1,2,0:T(4,128)S(1)}, u32[]{:S(2)}, u32[]{:S(2)}) async-start(f32[32,32,3]{1,2,0:T(4,128)} %copy.63), calls=%async_computation.3 | async-start | bytes 131072 | tf_op jit(solution)/shard_map/all_to_all | solution.py:70
  64.2 11.4 %all-to-all-start.2 = ((f32[32,32,3]{1,2,0:T(4,128)}), f32[32,32,3]{1,2,0:T(4,128)S(1)}, u32[]{:S(2)}, u32[]{:S(2)}) async-start(f32[32,32,3]{1,2,0:T(4,128)} %copy.59), calls=%async_computation.2 | async-start | bytes 131072 | tf_op jit(solution)/shard_map/all_to_all | solution.py:69
  73.7 7.7 %copy-start.1 = (bf16[32,768]{1,0:T(8,128)(2,1)S(1)}, bf16[32,768]{1,0:T(8,128)(2,1)}, u32[]{:S(2)}) copy-start(bf16[32,768]{1,0:T(8,128)(2,1)} %param.9) | copy-start | bytes 147460
  73.7 7.7 %copy-start.4 = (bf16[32,512]{1,0:T(8,128)(2,1)S(1)}, bf16[32,512]{1,0:T(8,128)(2,1)}, u32[]{:S(2)}) copy-start(bf16[32,512]{1,0:T(8,128)(2,1)} %param.10) | copy-start | bytes 98308
  75.6 58.5 %all-to-all-start.1 = ((f32[1024,3,256]{2,1,0:T(4,128)}), f32[1024,3,256]{2,1,0:T(4,128)}, u32[]{:S(2)}, u32[]{:S(2)}) async-start(f32[1024,3,256]{2,1,0:T(4,128)} %copy.57), calls=%async_computation.1 | async-start | bytes 8388608 | tf_op jit(solution)/shard_map/all_to_all | solution.py:71
  81.3 99.8 %all-reduce.2.cloned.1.call-start = ((), (), s32[]{:S(2)}) async-start(), calls=%async_computation.4 | async-start | bytes 327680 | tf_op jit(solution)/shard_map/psum | solution.py:100
  134.1 3.4 %copy-start = (bf16[768,2560]{1,0:T(8,128)(2,1)S(1)}, bf16[768,2560]{1,0:T(8,128)(2,1)}, u32[]{:S(2)}) copy-start(bf16[768,2560]{1,0:T(8,128)(2,1)} %param.12) | copy-start | bytes 11796484
  134.1 47.1 %copy-start.2 = (bf16[32,640]{1,0:T(8,128)(2,1)S(1)}, bf16[32,640]{1,0:T(8,128)(2,1)}, u32[]{:S(2)}) copy-start(bf16[32,640]{1,0:T(8,128)(2,1)} %param.8) | copy-start | bytes 122884
Sparse Core Ops, SparseCore 0:
  139.1 42.0 all-reduce.1
